TPU v7x, 32 devices: a whole 2x2x4 slice. The times are simulated.
32 devices in a mesh: shot: 2 (over core), gy: 4 (over y, x), gx: 4 (over z).
Axes of the slice: x: 2, y: 2, z: 4, core: 2. Of those that a mesh axis runs over, the one named last changes fastest.
Arguments:
- fwd_prev: float32 [2, 4, 1024, 512], P('shot', None, 'gy', 'gx'), may hold values from -6 to 6
- fwd_cur: float32 [2, 4, 1024, 512], P('shot', None, 'gy', 'gx'), may hold values from -6 to 6
- adj_late: float32 [2, 4, 1024, 512], P('shot', None, 'gy', 'gx'), may hold values from -6 to 6
- adj_now: float32 [2, 4, 1024, 512], P('shot', None, 'gy', 'gx'), may hold values from -6 to 6
- courant: float32 [4, 1024, 512], P(None, 'gy', 'gx'), may hold values from 0.02 to 0.19
- wavelet: float32 [2, 2], P('shot'), may hold values from -16 to 16
- boxes: int32 [2, 4], P('shot'), may hold values from 0 to 1024, as said below
- sources: int32 [2, 3], P('shot'), may hold values from 0 to 1023, as said below
- slab_top: int32 [1], replicated, may hold values from 0 to 508
Outputs:
- gradient: float32 [2, 512, 256], P(None, 'gy', 'gx')
Inputs may be any that keep to these rules, and one draw needn't show every extreme that they name: `boxes`: shot s's box is y0 <= y < y1, x0 <= x < x1 with y0 < y1 <= 1024, x0 < x1 <= 512, every bound a multiple of 16. `sources`: each shot's source cell (z, y, x) lies in the slab and inside that shot's box.
All inputs are finite; a program needn't handle non-finite values.
Results may differ from a plain program's by a relative error of at most 0.0003.
Values sent between devices are 32-bit elements; how exact they have to be, the bound alone decides.
A program may use at most 128 MiB of HBM per device.

v0:
```python
import jax
import jax.numpy as jnp
from jax import lax
from jax.sharding import PartitionSpec as P

COEFFS = (-205.0 / 72.0, 8.0 / 5.0, -1.0 / 5.0, 8.0 / 315.0, -1.0 / 560.0)


def with_halo(cells, sides, width):
    for axis, dim in sides:
        count = lax.axis_size(axis)
        ends = count - 1
        head = lax.slice_in_dim(cells, 0, width, axis=dim)
        tail = lax.slice_in_dim(cells, cells.shape[dim] - width, cells.shape[dim], axis=dim)
        cells = jnp.concatenate(
            [
                lax.ppermute(tail, axis, [(i, (i + 1) % count) for i in range(ends)]),
                cells,
                lax.ppermute(head, axis, [((i + 1) % count, i) for i in range(ends)]),
            ],
            axis=dim,
        )
    return cells


def stencil(padded):
    depth_count = padded.shape[1]
    out_y = padded.shape[2] - 8
    out_x = padded.shape[3] - 8
    deep_pad = jnp.pad(padded[:, :, 4 : 4 + out_y, 4 : 4 + out_x], ((0, 0), (4, 4), (0, 0), (0, 0)))
    summed = 3.0 * COEFFS[0] * deep_pad[:, 4 : 4 + depth_count]
    for offset in range(1, 5):
        neighbours = (
            deep_pad[:, 4 + offset : 4 + offset + depth_count]
            + deep_pad[:, 4 - offset : 4 - offset + depth_count]
        )
        neighbours = neighbours + padded[:, :, 4 + offset : 4 + offset + out_y, 4 : 4 + out_x]
        neighbours = neighbours + padded[:, :, 4 - offset : 4 - offset + out_y, 4 : 4 + out_x]
        neighbours = neighbours + padded[:, :, 4 : 4 + out_y, 4 + offset : 4 + offset + out_x]
        neighbours = neighbours + padded[:, :, 4 : 4 + out_y, 4 - offset : 4 - offset + out_x]
        summed = summed + COEFFS[offset] * neighbours
    return summed


def per_device(fwd_prev, fwd_cur, adj_late, adj_now, courant, wavelet, boxes, sources, slab_top):
    shot_count, depth_count, span_y, span_x = fwd_cur.shape
    anchor_y = lax.axis_index("gy") * span_y
    anchor_x = lax.axis_index("gx") * span_x
    boxes_twice = jnp.concatenate([boxes, boxes], 0)

    def box_mask(margin, box_rows):
        cells_y = anchor_y - margin + jnp.arange(span_y + 2 * margin, dtype=jnp.int32)
        cells_x = anchor_x - margin + jnp.arange(span_x + 2 * margin, dtype=jnp.int32)
        inside_y = (
            (cells_y[None, :] >= box_rows[:, 0:1]) & (cells_y[None, :] < box_rows[:, 1:2])
        ).astype(jnp.float32)
        inside_x = (
            (cells_x[None, :] >= box_rows[:, 2:3]) & (cells_x[None, :] < box_rows[:, 3:4])
        ).astype(jnp.float32)
        return inside_y[:, None, :, None] * inside_x[:, None, None, :]

    def source_term(margin, column):
        cells_y = anchor_y - margin + jnp.arange(span_y + 2 * margin, dtype=jnp.int32)
        cells_x = anchor_x - margin + jnp.arange(span_x + 2 * margin, dtype=jnp.int32)
        cells_z = jnp.arange(depth_count, dtype=jnp.int32)
        onehot_z = (cells_z[None, :] == sources[:, 0:1]).astype(jnp.float32)
        onehot_y = (cells_y[None, :] == sources[:, 1:2]).astype(jnp.float32)
        onehot_x = (cells_x[None, :] == sources[:, 2:3]).astype(jnp.float32)
        weighted = onehot_z * wavelet[:, column : column + 1]
        source_field = (
            weighted[:, :, None, None] * onehot_y[:, None, :, None] * onehot_x[:, None, None, :]
        )
        source_field = jnp.concatenate([source_field, jnp.zeros_like(source_field)], 0)
        return source_field

    stacked_before = jnp.concatenate([fwd_prev, adj_late, courant[None]], 0)
    current = jnp.concatenate([fwd_cur, adj_now], 0)
    older_wide = with_halo(stacked_before, (("gy", 2), ("gx", 3)), 4)
    newer_wide = with_halo(current, (("gy", 2), ("gx", 3)), 8)
    speed_wide = older_wide[2 * shot_count :]
    update = (
        2.0 * newer_wide[:, :, 4:-4, 4:-4]
        - older_wide[: 2 * shot_count]
        + speed_wide * stencil(newer_wide)
    )
    update = update + source_term(4, 0)
    middle = box_mask(4, boxes_twice) * update
    interior = middle[:, :, 4:-4, 4:-4]
    update = 2.0 * interior - current + courant * stencil(middle)
    update = update + source_term(0, 1)
    latest = box_mask(0, boxes_twice) * update
    fwd_mid, adj_mid = (interior[:shot_count], interior[shot_count:])
    fwd_last, adj_first = (latest[:shot_count], latest[shot_count:])
    image_cell = adj_first * (fwd_mid - 2.0 * fwd_cur + fwd_prev) + adj_mid * (
        fwd_last - 2.0 * fwd_mid + fwd_cur
    )
    coarse = image_cell.reshape(
        shot_count, depth_count // 2, 2, span_y // 2, 2, span_x // 2, 2
    ).mean(axis=(2, 4, 6))
    coarse = jnp.sum(coarse, axis=0)
    depth_index = (
        slab_top[0].astype(jnp.float32)
        + 2.0 * jnp.arange(depth_count // 2).astype(jnp.float32)
        + 1.0
    )
    factor = (0.25 + depth_index / 128.0)[:, None, None]
    total = lax.psum(coarse, "shot")
    return total * factor


def solution(mesh):
    return jax.shard_map(
        per_device,
        mesh=mesh,
        in_specs=(
            P("shot", None, "gy", "gx"),
            P("shot", None, "gy", "gx"),
            P("shot", None, "gy", "gx"),
            P("shot", None, "gy", "gx"),
            P(None, "gy", "gx"),
            P("shot", None),
            P("shot", None),
            P("shot", None),
            P(),
        ),
        out_specs=P(None, "gy", "gx"),
        check_vma=False,
    )
```

profile of v0, /device:TPU:0, one launch (start us, length us, event | category | flops | bytes accessed | tf_op | source)
XLA Modules:
  0.0 153.4 jit_solution(927272376209038710)
XLA Ops:
  6.5 1.3 copy.38
  7.8 1.2 copy.39
  10.0 5.0 %collective-permute-start.4 = (f32[3,4,4,128]{3,2,1,0:T(4,128)S(1)}, f32[3,4,4,128]{3,2,1,0:T(4,128)S(1)}, u32[]{:S(2)}, u32[]{:S(2)}) collective-permute-start(f32[3,4,4,128]{3,2,1,0:T(4,128)S(1)} %copy.41), channel_id=1, source_target_pairs={{0,4},{4,8},{8,12},{1,5},{5,9},{9,13},{2,6},{6,10},{10,14},{3,7},{... | collective-permute-start | bytes 73736 | tf_op jit(solution)/shard_map/ppermute | solution.py:17
  15.3 1.3 collective-permute-start.5
  16.6 1.2 copy.36
  18.1 1.1 fusion.57
  19.2 5.3 %collective-permute-start = (f32[2,4,8,128]{2,3,1,0:T(8,128)}, f32[2,4,8,128]{2,3,1,0:T(8,128)}, u32[]{:S(2)}, u32[]{:S(2)}) collective-permute-start(f32[2,4,8,128]{2,3,1,0:T(8,128)} %get-tuple-element.15), channel_id=1, source_target_pairs={{0,4},{4,8},{8,12},{1,5},{5,9},{9,13},{2,6},{6,10},{10,14},{3,7},{... | collective-permute-start | bytes 98312 | tf_op jit(solution)/shard_map/ppermute | solution.py:17
  24.5 1.3 collective-permute-start.1
  30.1 0.9 broadcast_multiply_fusion.2
  30.9 1.8 %compare_select_fusion = (f32[4]{0:T(128)S(1)}, f32[4]{0:T(128)S(1)}) fusion(f32[]{:T(128)} %bitcast.6, s32[]{:T(128)} %bitcast.2, f32[]{:T(128)} %bitcast.3), kind=kLoop, calls=%fused_computation.124 | loop fusion | flops 12 | bytes 44 | tf_op jit(solution)/shard_map/mul | solution.py:69
  32.8 1.0 broadcast_multiply_fusion
  33.9 0.9 broadcast_multiply_fusion.1
  34.9 0.8 broadcast_multiply_fusion.3
  36.6 1.2 copy.44
  37.8 1.0 pad_maximum_fusion.20
  38.8 3.6 %collective-permute-start.6 = (f32[3,4,264,4]{2,3,1,0:T(4,128)S(1)}, f32[3,4,264,4]{2,3,1,0:T(4,128)S(1)}, u32[]{:S(2)}, u32[]{:S(2)}) collective-permute-start(f32[3,4,264,4]{2,3,1,0:T(4,128)S(1)} %get-tuple-element.9), channel_id=1, source_target_pairs={{0,1},{1,2},{2,3},{4,5},{5,6},{6,7},{8,9},{9,10},{10,11},{12,13},{... | collective-permute-start | bytes 152072 | tf_op jit(solution)/shard_map/ppermute | solution.py:17
  42.5 1.3 collective-permute-start.7
  43.8 5.0 %collective-permute-done.1 = f32[2,4,8,128]{2,3,1,0:T(8,128)} collective-permute-done((f32[2,4,8,128]{2,3,1,0:T(8,128)}, f32[2,4,8,128]{2,3,1,0:T(8,128)}, u32[]{:S(2)}, u32[]{:S(2)}) %collective-permute-start.1) | collective-permute-done | bytes 32800 | tf_op jit(solution)/shard_map/ppermute | solution.py:19
  48.7 0.9 pad_maximum_fusion.12
  49.7 3.5 %collective-permute-start.2 = (f32[2,4,272,8]{2,3,1,0:T(8,128)S(1)}, f32[2,4,272,8]{2,3,1,0:T(8,128)S(1)}, u32[]{:S(2)}, u32[]{:S(2)}) collective-permute-start(f32[2,4,272,8]{2,3,1,0:T(8,128)S(1)} %get-tuple-element.12), channel_id=1, source_target_pairs={{0,1},{1,2},{2,3},{4,5},{5,6},{6,7},{8,9},{9,10},{10,11},{12,13},{... | collective-permute-start | bytes 208904 | tf_op jit(solution)/shard_map/ppermute | solution.py:17
  53.2 1.5 collective-permute-start.3
  54.7 2.5 %pad_maximum_fusion = f32[3,4,264,136]{2,3,1,0:T(8,128)} fusion(f32[3,4,264,4]{2,3,1,0:T(4,128)S(1)} %collective-permute-done.7, f32[3,4,4,128]{2,3,1,0:T(8,128)S(1)} %copy-done, f32[1,4,256,128]{2,3,1,0:T(8,128)S(1)} %bitcast.13, f32[1,4,256,128]{2,3,1,0:T(8,128)S(1)} %copy.40, f32[1,4,256,128]{2,3,1,0:T(8,128)S(1)} %copy.39, ...), kind=kLoop, calls=%fused_computation.12 | loop fusion | flops 2585088 | bytes 3446784 | tf_op jit(solution)/shard_map/concatenate | solution.py:15
  57.2 1.3 maximum_bitcast_fusion
  58.4 1.2 collective-permute-done.3
  60.3 1.8 %pad_maximum_fusion.1 = f32[2,4,272,144]{2,3,1,0:T(8,128)S(1)} fusion(f32[2,4,272,8]{2,3,1,0:T(8,128)S(1)} %collective-permute-done.3, f32[2,4,8,128]{2,3,1,0:T(8,128)} %collective-permute-done.1, f32[1,4,256,128]{2,3,1,0:T(8,128)S(1)} %copy.37, f32[1,4,256,128]{2,3,1,0:T(8,128)S(1)} %copy.36, f32[2,4,8,128]{2,3,1,0:T(8,128)} %collective-permute-done, ...), kind=kLoop, calls=%fused_computation.13 | loop fusion | flops 1566720 | bytes 2506752 | tf_op jit(solution)/shard_map/concatenate | solution.py:15
  63.2 10.9 %fusion.28 = f32[2,4,264,136]{2,3,1,0:T(8,128)S(1)} fusion(f32[1,4,264,136]{2,3,1,0:T(8,128)} %broadcast_multiply_fusion, f32[2,4,8,128]{2,3,1,0:T(8,128)} %collective-permute-done.1, f32[1,4,256,128]{2,3,1,0:T(8,128)S(1)} %copy.37, f32[1,4,256,128]{2,3,1,0:T(8,128)S(1)} %copy.36, f32[2,4,8,128]{2,3,1,0:T(8,128)} %collective-permute-done, ...), kind=kLoop, calls=%fused_computation.52 | loop fusion | flops 11776512 | bytes 22221312 | tf_op jit(solution)/shard_map/mul | solution.py:87
  74.4 0.7 copy-done.1
  75.2 4.3 %fusion.32 = f32[2,4,256,128]{2,3,1,0:T(8,128)S(1)} fusion(f32[1,4,256,128]{2,3,1,0:T(8,128)S(1)} %copy.37, f32[1,4,256,128]{2,3,1,0:T(8,128)S(1)} %copy.36, f32[2,4,256,128]{2,3,1,0:T(8,128)S(1)} %slice.317, f32[2,4,264,136]{2,3,1,0:T(8,128)S(1)} %fusion.28, f32[1,4,256,128]{2,3,1,0:T(8,128)S(1)} %copy-done.1, f32[4,256,128]{1,2,0:T(8,128)S(1)} %copy.38, ...), kind=kLoop, calls=%fused_computation.62 | loop fusion | flops 8912896 | bytes 21233664 | tf_op jit(solution)/shard_map/mul | solution.py:91
  80.1 34.8 %reshape.410 = f32[2,2,128,2,64,2]{5,4,3,2,1,0:T(8,128)} reshape(f32[1,4,256,128]{3,2,1,0:T(8,128)S(1)} %copy.49) | data formatting | bytes 1048576 | tf_op jit(solution)/shard_map/reshape | solution.py:97
  114.9 12.2 %reduce_sum.8 = f32[2,128,64]{2,1,0:T(8,128)S(1)} reduce(f32[2,2,128,2,64,2]{5,4,3,2,1,0:T(8,128)} %reshape.410, f32[]{:T(128)} %constant.23.clone.1), dimensions={1,3,5}, to_apply=%region_0.1 | reduce | flops 114688 | bytes 589828 | tf_op jit(solution)/shard_map/reduce_sum | solution.py:99
  127.9 17.1 %all-reduce.6.cloned.1.call-done = f32[2,128,64]{1,2,0:T(8,128)} async-done(((f32[2,128,64]{1,2,0:T(8,128)}), f32[2,128,64]{1,2,0:T(8,128)}) %all-reduce.6.cloned.1.call-update) | async-done | bytes 65552 | tf_op jit(solution)/shard_map/psum | solution.py:107
  145.0 1.5 %broadcast_multiply_fusion.4 = f32[2,128,64]{1,2,0:T(8,128)} fusion(f32[2,128,64]{1,2,0:T(8,128)} %all-reduce.6.cloned.1.call-done, f32[2]{0:T(128)S(1)} %multiply_add_fusion), kind=kLoop, calls=%fused_computation.111 | loop fusion | flops 16384 | bytes 131080 | tf_op jit(solution)/shard_map/mul | solution.py:108
  (61 shorter events, 9.4 us)
Async XLA Ops:
  6.5 2.6 %copy-start.4 = (f32[1,4,256,128]{3,2,1,0:T(8,128)S(1)}, f32[1,4,256,128]{3,2,1,0:T(8,128)}, u32[]{:S(2)}) copy-start(f32[1,4,256,128]{3,2,1,0:T(8,128)} %param.11) | copy-start | bytes 1572868
  6.5 138.5 %all-reduce.6.cloned.1.call-start = ((), (), s32[]{:S(2)}) async-start(), calls=%async_computation | async-start | bytes 131072 | tf_op jit(solution)/shard_map/psum | solution.py:107
  10.0 7.8 %copy-start.5 = (f32[1,4,256,128]{3,2,1,0:T(8,128)S(1)}, f32[1,4,256,128]{3,2,1,0:T(8,128)}, u32[]{:S(2)}) copy-start(f32[1,4,256,128]{3,2,1,0:T(8,128)} %param.12) | copy-start | bytes 1572868
  10.0 26.3 %collective-permute-start.4 = (f32[3,4,4,128]{3,2,1,0:T(4,128)S(1)}, f32[3,4,4,128]{3,2,1,0:T(4,128)S(1)}, u32[]{:S(2)}, u32[]{:S(2)}) collective-permute-start(f32[3,4,4,128]{3,2,1,0:T(4,128)S(1)} %copy.41), channel_id=1, source_target_pairs={{0,4},{4,8},{8,12},{1,5},{5,9},{9,13},{2,6},{6,10},{10,14},{3,7},{... | collective-permute-start | bytes 73736 | tf_op jit(solution)/shard_map/ppermute | solution.py:17
  15.3 21.3 %collective-permute-start.5 = (f32[3,4,4,128]{3,2,1,0:T(4,128)S(1)}, f32[3,4,4,128]{3,2,1,0:T(4,128)S(1)}, u32[]{:S(2)}, u32[]{:S(2)}) collective-permute-start(f32[3,4,4,128]{3,2,1,0:T(4,128)S(1)} %copy.42), channel_id=1, source_target_pairs={{4,0},{8,4},{12,8},{5,1},{9,5},{13,9},{6,2},{10,6},{14,10},{7,3},{... | collective-permute-start | bytes 73736 | tf_op jit(solution)/shard_map/ppermute | solution.py:19
  17.8 8.0 %copy-start.8 = (s32[1,3]{1,0:T(1,128)S(1)}, s32[1,3]{1,0:T(1,128)}, u32[]{:S(2)}) copy-start(s32[1,3]{1,0:T(1,128)} %param.16) | copy-start | bytes 40
  17.9 11.1 %copy-start.10 = (s32[1,4]{1,0:T(1,128)S(1)}, s32[1,4]{1,0:T(1,128)}, u32[]{:S(2)}) copy-start(s32[1,4]{1,0:T(1,128)} %param.15) | copy-start | bytes 52
  17.9 11.3 %copy-start.9 = (f32[1,2]{1,0:T(1,128)S(1)}, f32[1,2]{1,0:T(1,128)}, u32[]{:S(2)}) copy-start(f32[1,2]{1,0:T(1,128)} %param.14) | copy-start | bytes 28
  19.2 24.6 %collective-permute-start = (f32[2,4,8,128]{2,3,1,0:T(8,128)}, f32[2,4,8,128]{2,3,1,0:T(8,128)}, u32[]{:S(2)}, u32[]{:S(2)}) collective-permute-start(f32[2,4,8,128]{2,3,1,0:T(8,128)} %get-tuple-element.15), channel_id=1, source_target_pairs={{0,4},{4,8},{8,12},{1,5},{5,9},{9,13},{2,6},{6,10},{10,14},{3,7},{... | collective-permute-start | bytes 98312 | tf_op jit(solution)/shard_map/ppermute | solution.py:17
  24.5 24.2 %collective-permute-start.1 = (f32[2,4,8,128]{2,3,1,0:T(8,128)}, f32[2,4,8,128]{2,3,1,0:T(8,128)}, u32[]{:S(2)}, u32[]{:S(2)}) collective-permute-start(f32[2,4,8,128]{2,3,1,0:T(8,128)} %get-tuple-element.16), channel_id=1, source_target_pairs={{4,0},{8,4},{12,8},{5,1},{9,5},{13,9},{6,2},{10,6},{14,10},{7,3},{... | collective-permute-start | bytes 98312 | tf_op jit(solution)/shard_map/ppermute | solution.py:19
  38.8 15.9 %copy-start = (f32[3,4,4,128]{2,3,1,0:T(8,128)S(1)}, f32[3,4,4,128]{2,3,1,0:T(8,128)}, u32[]{:S(2)}) copy-start(f32[3,4,4,128]{2,3,1,0:T(8,128)} %copy.44) | copy-start | bytes 73732
  38.8 15.8 %collective-permute-start.6 = (f32[3,4,264,4]{2,3,1,0:T(4,128)S(1)}, f32[3,4,264,4]{2,3,1,0:T(4,128)S(1)}, u32[]{:S(2)}, u32[]{:S(2)}) collective-permute-start(f32[3,4,264,4]{2,3,1,0:T(4,128)S(1)} %get-tuple-element.9), channel_id=1, source_target_pairs={{0,1},{1,2},{2,3},{4,5},{5,6},{6,7},{8,9},{9,10},{10,11},{12,13},{... | collective-permute-start | bytes 152072 | tf_op jit(solution)/shard_map/ppermute | solution.py:17
  42.5 12.2 %collective-permute-start.7 = (f32[3,4,264,4]{2,3,1,0:T(4,128)S(1)}, f32[3,4,264,4]{2,3,1,0:T(4,128)S(1)}, u32[]{:S(2)}, u32[]{:S(2)}) collective-permute-start(f32[3,4,264,4]{2,3,1,0:T(4,128)S(1)} %get-tuple-element.10), channel_id=1, source_target_pairs={{1,0},{2,1},{3,2},{5,4},{6,5},{7,6},{9,8},{10,9},{11,10},{13,12},{... | collective-permute-start | bytes 152072 | tf_op jit(solution)/shard_map/ppermute | solution.py:19
  49.7 8.8 %collective-permute-start.2 = (f32[2,4,272,8]{2,3,1,0:T(8,128)S(1)}, f32[2,4,272,8]{2,3,1,0:T(8,128)S(1)}, u32[]{:S(2)}, u32[]{:S(2)}) collective-permute-start(f32[2,4,272,8]{2,3,1,0:T(8,128)S(1)} %get-tuple-element.12), channel_id=1, source_target_pairs={{0,1},{1,2},{2,3},{4,5},{5,6},{6,7},{8,9},{9,10},{10,11},{12,13},{... | collective-permute-start | bytes 208904 | tf_op jit(solution)/shard_map/ppermute | solution.py:17
  53.2 6.5 %collective-permute-start.3 = (f32[2,4,272,8]{2,3,1,0:T(8,128)S(1)}, f32[2,4,272,8]{2,3,1,0:T(8,128)S(1)}, u32[]{:S(2)}, u32[]{:S(2)}) collective-permute-start(f32[2,4,272,8]{2,3,1,0:T(8,128)S(1)} %get-tuple-element.11), channel_id=1, source_target_pairs={{1,0},{2,1},{3,2},{5,4},{6,5},{7,6},{9,8},{10,9},{11,10},{13,12},{... | collective-permute-start | bytes 208904 | tf_op jit(solution)/shard_map/ppermute | solution.py:19
  59.7 0.6 copy-start.6
  62.1 1.0 copy-start.2
  62.2 1.0 copy-start.7
  74.1 1.0 copy-start.1
  74.1 1.1 copy-start.3
Sparse Core Ops, SparseCore 0:
  128.1 16.9 all-reduce.5
where the time goes:
time: 154 us; the launch traced here: 153 us
  other arithmetic  47.1 us (31%)
  local copies, waits for them, and re-layouts  45.7 us (30%)
  waiting for transfers between devices  23.3 us (15%)
  starting transfers between devices  22.8 us (15%)
  between operations  14.5 us (9%)
    reshape x1, local copies, waits for them, and re-layouts, per_device(): image_cell.reshape(shot_count, depth_count // 2, 2, span_y // 2, 2, span_...  34.8 us
    ppermute x4, starting transfers between devices, with_halo(): lax.ppermute(tail, axis, [(i, (i + 1) % count) for i in range(ends)])  17.4 us
    psum x1, waiting for transfers between devices, per_device(): total = lax.psum(coarse, 'shot')  17.1 us
    reduce_sum x1, other arithmetic, per_device(): coarse = image_cell.reshape(shot_count, depth_count // 2, 2, span_y // 2,...  12.2 us
    mul x1, other arithmetic, per_device(): middle = box_mask(4, boxes_twice) * update  10.9 us
    ppermute x4, waiting for transfers between devices, with_halo(): lax.ppermute(head, axis, [((i + 1) % count, i) for i in range(ends)])  6.23 us
    unnamed x27, local copies, waits for them, and re-layouts  5.99 us
    ppermute x4, starting transfers between devices, with_halo(): lax.ppermute(head, axis, [((i + 1) % count, i) for i in range(ends)])  5.34 us
  transfers between devices with their start and end apart: 9, of which 3 were waited for; matrix products, arithmetic and copies ran while one was open for 13% of the time, Pallas kernels for 0%

commit v1 on v0

--- a/solution.py
+++ b/solution.py
@@ -104,7 +104,7 @@
         + 1.0
     )
     factor = (0.25 + depth_index / 128.0)[:, None, None]
-    total = lax.psum(coarse, "shot")
+    total = jnp.sum(lax.all_gather(coarse, "shot"), axis=0)
     return total * factor
 
 

time: 154 us -> 124 us (0.81)
  waiting for transfers between devices: 23.3 us -> 5.86 us
  between operations: 14.5 us -> 1.09 us
  blocking collectives: 0 us -> 1.9 us
    psum x1 -> x0, waiting for transfers between devices: 17.1 us -> none  [per_device(): total = lax.psum(coarse, 'shot')]
    all_gather x0 -> x1, blocking collectives: none -> 1.9 us  [per_device(): total = jnp.sum(lax.all_gather(coarse, 'shot'), axis=0)]
  transfers between devices with their start and end apart: 9 -> 8, of which waited for: 3 -> 2; matrix products, arithmetic and copies ran while one was open for 13% -> 16% of each run, Pallas kernels for 0% -> 0%
where the time goes in v1:
time: 124 us; the launch traced here: 123 us
  other arithmetic  46 us (37%)
  local copies, waits for them, and re-layouts  45.8 us (37%)
  starting transfers between devices  22.8 us (18%)
  waiting for transfers between devices  5.86 us (5%)
  blocking collectives  1.9 us (2%)
    reshape x1, local copies, waits for them, and re-layouts, per_device(): image_cell.reshape(shot_count, depth_count // 2, 2, span_y // 2, 2, span_...  34.8 us
    ppermute x4, starting transfers between devices, with_halo(): lax.ppermute(tail, axis, [(i, (i + 1) % count) for i in range(ends)])  17.4 us
    reduce_sum x1, other arithmetic, per_device(): coarse = image_cell.reshape(shot_count, depth_count // 2, 2, span_y // 2,...  12.2 us
    mul x1, other arithmetic, per_device(): middle = box_mask(4, boxes_twice) * update  10.9 us
    unnamed x27, local copies, waits for them, and re-layouts  5.99 us
    ppermute x4, waiting for transfers between devices, with_halo(): lax.ppermute(head, axis, [((i + 1) % count, i) for i in range(ends)])  5.85 us
    ppermute x4, starting transfers between devices, with_halo(): lax.ppermute(head, axis, [((i + 1) % count, i) for i in range(ends)])  5.34 us
    concatenate x3, other arithmetic, with_halo(): jnp.concatenate([lax.ppermute(tail, axis, [(i, (i + 1) % count) for i in...  5.2 us
  transfers between devices with their start and end apart: 8, of which 2 were waited for; matrix products, arithmetic and copies ran while one was open for 16% of the time, Pallas kernels for 0%

profile of v1, /device:TPU:0, one launch (start us, length us, event | category | flops | bytes accessed | tf_op | source)
XLA Modules:
  0.0 123.4 jit_solution(15373923425586023670)
XLA Ops:
  0.0 1.3 %copy.37 = f32[4,256,128]{1,2,0:T(8,128)S(1)} copy(f32[4,256,128]{2,1,0:T(8,128)} %param.13) | data formatting | bytes 1048576 | tf_op args[4]
  1.3 1.2 %copy.38 = f32[1,4,256,128]{2,3,1,0:T(8,128)S(1)} copy(f32[1,4,256,128]{3,2,1,0:T(8,128)} %param.9) | data formatting | bytes 1048576 | tf_op args[0]
  3.5 5.0 %collective-permute-start.4 = (f32[3,4,4,128]{3,2,1,0:T(4,128)S(1)}, f32[3,4,4,128]{3,2,1,0:T(4,128)S(1)}, u32[]{:S(2)}, u32[]{:S(2)}) collective-permute-start(f32[3,4,4,128]{3,2,1,0:T(4,128)S(1)} %copy.40), channel_id=1, source_target_pairs={{0,4},{4,8},{8,12},{1,5},{5,9},{9,13},{2,6},{6,10},{10,14},{3,7},{... | collective-permute-start | bytes 73736 | tf_op jit(solution)/shard_map/ppermute | solution.py:17
  8.8 1.3 %collective-permute-start.5 = (f32[3,4,4,128]{3,2,1,0:T(4,128)S(1)}, f32[3,4,4,128]{3,2,1,0:T(4,128)S(1)}, u32[]{:S(2)}, u32[]{:S(2)}) collective-permute-start(f32[3,4,4,128]{3,2,1,0:T(4,128)S(1)} %copy.41), channel_id=1, source_target_pairs={{4,0},{8,4},{12,8},{5,1},{9,5},{13,9},{6,2},{10,6},{14,10},{7,3},{... | collective-permute-start | bytes 73736 | tf_op jit(solution)/shard_map/ppermute | solution.py:19
  10.1 1.2 %copy.35 = f32[1,4,256,128]{2,3,1,0:T(8,128)S(1)} copy(f32[1,4,256,128]{3,2,1,0:T(8,128)} %param.10) | data formatting | bytes 1048576 | tf_op args[1]
  11.5 1.1 fusion.57
  12.7 5.3 %collective-permute-start = (f32[2,4,8,128]{2,3,1,0:T(8,128)}, f32[2,4,8,128]{2,3,1,0:T(8,128)}, u32[]{:S(2)}, u32[]{:S(2)}) collective-permute-start(f32[2,4,8,128]{2,3,1,0:T(8,128)} %get-tuple-element.15), channel_id=1, source_target_pairs={{0,4},{4,8},{8,12},{1,5},{5,9},{9,13},{2,6},{6,10},{10,14},{3,7},{... | collective-permute-start | bytes 98312 | tf_op jit(solution)/shard_map/ppermute | solution.py:17
  18.0 1.3 %collective-permute-start.1 = (f32[2,4,8,128]{2,3,1,0:T(8,128)}, f32[2,4,8,128]{2,3,1,0:T(8,128)}, u32[]{:S(2)}, u32[]{:S(2)}) collective-permute-start(f32[2,4,8,128]{2,3,1,0:T(8,128)} %get-tuple-element.16), channel_id=1, source_target_pairs={{4,0},{8,4},{12,8},{5,1},{9,5},{13,9},{6,2},{10,6},{14,10},{7,3},{... | collective-permute-start | bytes 98312 | tf_op jit(solution)/shard_map/ppermute | solution.py:19
  21.3 0.7 compare_convert_fusion.2
  24.5 0.9 broadcast_multiply_fusion.2
  25.4 1.9 %compare_select_fusion = (f32[4]{0:T(128)S(1)}, f32[4]{0:T(128)S(1)}) fusion(f32[]{:T(128)} %bitcast.6, s32[]{:T(128)} %bitcast.2, f32[]{:T(128)} %bitcast.3), kind=kLoop, calls=%fused_computation.124 | loop fusion | flops 12 | bytes 44 | tf_op jit(solution)/shard_map/mul | solution.py:69
  27.3 1.0 broadcast_multiply_fusion
  28.4 0.8 broadcast_multiply_fusion.3
  29.3 0.9 broadcast_multiply_fusion.1
  30.5 1.2 copy.43
  31.7 1.0 pad_maximum_fusion.20
  32.7 3.6 %collective-permute-start.6 = (f32[3,4,264,4]{2,3,1,0:T(4,128)S(1)}, f32[3,4,264,4]{2,3,1,0:T(4,128)S(1)}, u32[]{:S(2)}, u32[]{:S(2)}) collective-permute-start(f32[3,4,264,4]{2,3,1,0:T(4,128)S(1)} %get-tuple-element.9), channel_id=1, source_target_pairs={{0,1},{1,2},{2,3},{4,5},{5,6},{6,7},{8,9},{9,10},{10,11},{12,13},{... | collective-permute-start | bytes 152072 | tf_op jit(solution)/shard_map/ppermute | solution.py:17
  36.3 1.3 %collective-permute-start.7 = (f32[3,4,264,4]{2,3,1,0:T(4,128)S(1)}, f32[3,4,264,4]{2,3,1,0:T(4,128)S(1)}, u32[]{:S(2)}, u32[]{:S(2)}) collective-permute-start(f32[3,4,264,4]{2,3,1,0:T(4,128)S(1)} %get-tuple-element.10), channel_id=1, source_target_pairs={{1,0},{2,1},{3,2},{5,4},{6,5},{7,6},{9,8},{10,9},{11,10},{13,12},{... | collective-permute-start | bytes 152072 | tf_op jit(solution)/shard_map/ppermute | solution.py:19
  37.6 4.6 %collective-permute-done.1 = f32[2,4,8,128]{2,3,1,0:T(8,128)} collective-permute-done((f32[2,4,8,128]{2,3,1,0:T(8,128)}, f32[2,4,8,128]{2,3,1,0:T(8,128)}, u32[]{:S(2)}, u32[]{:S(2)}) %collective-permute-start.1) | collective-permute-done | bytes 32800 | tf_op jit(solution)/shard_map/ppermute | solution.py:19
  42.2 0.9 pad_maximum_fusion.12
  43.2 3.5 %collective-permute-start.2 = (f32[2,4,272,8]{2,3,1,0:T(8,128)S(1)}, f32[2,4,272,8]{2,3,1,0:T(8,128)S(1)}, u32[]{:S(2)}, u32[]{:S(2)}) collective-permute-start(f32[2,4,272,8]{2,3,1,0:T(8,128)S(1)} %get-tuple-element.12), channel_id=1, source_target_pairs={{0,1},{1,2},{2,3},{4,5},{5,6},{6,7},{8,9},{9,10},{10,11},{12,13},{... | collective-permute-start | bytes 208904 | tf_op jit(solution)/shard_map/ppermute | solution.py:17
  46.7 1.5 %collective-permute-start.3 = (f32[2,4,272,8]{2,3,1,0:T(8,128)S(1)}, f32[2,4,272,8]{2,3,1,0:T(8,128)S(1)}, u32[]{:S(2)}, u32[]{:S(2)}) collective-permute-start(f32[2,4,272,8]{2,3,1,0:T(8,128)S(1)} %get-tuple-element.11), channel_id=1, source_target_pairs={{1,0},{2,1},{3,2},{5,4},{6,5},{7,6},{9,8},{10,9},{11,10},{13,12},{... | collective-permute-start | bytes 208904 | tf_op jit(solution)/shard_map/ppermute | solution.py:19
  48.2 2.5 %pad_maximum_fusion = f32[3,4,264,136]{2,3,1,0:T(8,128)} fusion(f32[3,4,264,4]{2,3,1,0:T(4,128)S(1)} %collective-permute-done.7, f32[3,4,4,128]{2,3,1,0:T(8,128)S(1)} %copy-done, f32[1,4,256,128]{2,3,1,0:T(8,128)S(1)} %bitcast.14, f32[1,4,256,128]{2,3,1,0:T(8,128)S(1)} %copy.39, f32[1,4,256,128]{2,3,1,0:T(8,128)S(1)} %copy.38, ...), kind=kLoop, calls=%fused_computation.12 | loop fusion | flops 2585088 | bytes 3446784 | tf_op jit(solution)/shard_map/concatenate | solution.py:15
  50.6 1.3 %maximum_bitcast_fusion = f32[4,264,136]{1,2,0:T(8,128)} fusion(f32[3,4,264,4]{2,3,1,0:T(4,128)S(1)} %collective-permute-done.7, f32[3,4,264,4]{2,3,1,0:T(4,128)S(1)} %collective-permute-done.6, f32[3,4,4,128]{2,3,1,0:T(8,128)S(1)} %copy-done, f32[3,4,4,128]{2,3,1,0:T(8,128)S(1)} %copy.42, f32[1,4,256,128]{2,3,1,0:T(8,128)S(1)} %bitcast.15, ...), kind=kLoop, calls=%fused_computation.90 | loop fusion | flops 861696 | bytes 2297856 | tf_op jit(solution)/shard_map/mul | solution.py:84
  51.9 1.3 %collective-permute-done.3 = f32[2,4,272,8]{2,3,1,0:T(8,128)S(1)} collective-permute-done((f32[2,4,272,8]{2,3,1,0:T(8,128)S(1)}, f32[2,4,272,8]{2,3,1,0:T(8,128)S(1)}, u32[]{:S(2)}, u32[]{:S(2)}) %collective-permute-start.3) | collective-permute-done | bytes 69664 | tf_op jit(solution)/shard_map/ppermute | solution.py:19
  53.8 1.8 %pad_maximum_fusion.1 = f32[2,4,272,144]{2,3,1,0:T(8,128)S(1)} fusion(f32[2,4,272,8]{2,3,1,0:T(8,128)S(1)} %collective-permute-done.3, f32[2,4,8,128]{2,3,1,0:T(8,128)} %collective-permute-done.1, f32[1,4,256,128]{2,3,1,0:T(8,128)S(1)} %copy.36, f32[1,4,256,128]{2,3,1,0:T(8,128)S(1)} %copy.35, f32[2,4,8,128]{2,3,1,0:T(8,128)} %collective-permute-done, ...), kind=kLoop, calls=%fused_computation.13 | loop fusion | flops 1566720 | bytes 2506752 | tf_op jit(solution)/shard_map/concatenate | solution.py:15
  56.6 10.9 %fusion.28 = f32[2,4,264,136]{2,3,1,0:T(8,128)S(1)} fusion(f32[1,4,264,136]{2,3,1,0:T(8,128)} %broadcast_multiply_fusion, f32[2,4,8,128]{2,3,1,0:T(8,128)} %collective-permute-done.1, f32[1,4,256,128]{2,3,1,0:T(8,128)S(1)} %copy.36, f32[1,4,256,128]{2,3,1,0:T(8,128)S(1)} %copy.35, f32[2,4,8,128]{2,3,1,0:T(8,128)} %collective-permute-done, ...), kind=kLoop, calls=%fused_computation.52 | loop fusion | flops 11776512 | bytes 22221312 | tf_op jit(solution)/shard_map/mul | solution.py:87
  68.7 4.3 %fusion.32 = f32[2,4,256,128]{2,3,1,0:T(8,128)S(1)} fusion(f32[1,4,256,128]{2,3,1,0:T(8,128)S(1)} %copy.36, f32[1,4,256,128]{2,3,1,0:T(8,128)S(1)} %copy.35, f32[2,4,256,128]{2,3,1,0:T(8,128)S(1)} %slice.317, f32[2,4,264,136]{2,3,1,0:T(8,128)S(1)} %fusion.28, f32[1,4,256,128]{2,3,1,0:T(8,128)S(1)} %copy-done.1, f32[4,256,128]{1,2,0:T(8,128)S(1)} %copy.37, ...), kind=kLoop, calls=%fused_computation.62 | loop fusion | flops 8912896 | bytes 21233664 | tf_op jit(solution)/shard_map/mul | solution.py:91
  73.6 34.8 %reshape.418 = f32[2,2,128,2,64,2]{5,4,3,2,1,0:T(8,128)} reshape(f32[1,4,256,128]{3,2,1,0:T(8,128)S(1)} %copy.48) | data formatting | bytes 1048576 | tf_op jit(solution)/shard_map/reshape | solution.py:97
  108.4 12.2 %reduce_sum.16 = f32[2,128,64]{2,1,0:T(8,128)S(1)} reduce(f32[2,2,128,2,64,2]{5,4,3,2,1,0:T(8,128)} %reshape.418, f32[]{:T(128)} %constant.23.clone.1), dimensions={1,3,5}, to_apply=%region_0.1 | reduce | flops 114688 | bytes 589828 | tf_op jit(solution)/shard_map/reduce_sum | solution.py:99
  120.7 1.9 %all-gather = f32[4,128,64]{1,2,0:T(8,128)S(1)} all-gather(f32[2,128,64]{1,2,0:T(8,128)S(1)} %broadcast_multiply_fusion.5), channel_id=2, replica_groups=mesh['shot'=2,'gy'=4,'gx'=4] {'shot'}, dimensions={0}, use_global_device_ids=true | all-gather | bytes 196608 | tf_op jit(solution)/shard_map/all_gather | solution.py:107
  122.7 0.7 broadcast_multiply_fusion.4
  (60 shorter events, 9.1 us)
Async XLA Ops:
  0.0 2.6 %copy-start.4 = (f32[1,4,256,128]{3,2,1,0:T(8,128)S(1)}, f32[1,4,256,128]{3,2,1,0:T(8,128)}, u32[]{:S(2)}) copy-start(f32[1,4,256,128]{3,2,1,0:T(8,128)} %param.11) | copy-start | bytes 1572868
  3.5 7.8 %copy-start.5 = (f32[1,4,256,128]{3,2,1,0:T(8,128)S(1)}, f32[1,4,256,128]{3,2,1,0:T(8,128)}, u32[]{:S(2)}) copy-start(f32[1,4,256,128]{3,2,1,0:T(8,128)} %param.12) | copy-start | bytes 1572868
  3.5 26.7 %collective-permute-start.4 = (f32[3,4,4,128]{3,2,1,0:T(4,128)S(1)}, f32[3,4,4,128]{3,2,1,0:T(4,128)S(1)}, u32[]{:S(2)}, u32[]{:S(2)}) collective-permute-start(f32[3,4,4,128]{3,2,1,0:T(4,128)S(1)} %copy.40), channel_id=1, source_target_pairs={{0,4},{4,8},{8,12},{1,5},{5,9},{9,13},{2,6},{6,10},{10,14},{3,7},{... | collective-permute-start | bytes 73736 | tf_op jit(solution)/shard_map/ppermute | solution.py:17
  8.8 21.8 %collective-permute-start.5 = (f32[3,4,4,128]{3,2,1,0:T(4,128)S(1)}, f32[3,4,4,128]{3,2,1,0:T(4,128)S(1)}, u32[]{:S(2)}, u32[]{:S(2)}) collective-permute-start(f32[3,4,4,128]{3,2,1,0:T(4,128)S(1)} %copy.41), channel_id=1, source_target_pairs={{4,0},{8,4},{12,8},{5,1},{9,5},{13,9},{6,2},{10,6},{14,10},{7,3},{... | collective-permute-start | bytes 73736 | tf_op jit(solution)/shard_map/ppermute | solution.py:19
  11.3 8.0 %copy-start.8 = (s32[1,3]{1,0:T(1,128)S(1)}, s32[1,3]{1,0:T(1,128)}, u32[]{:S(2)}) copy-start(s32[1,3]{1,0:T(1,128)} %param.16) | copy-start | bytes 40
  11.3 11.3 %copy-start.10 = (s32[1,4]{1,0:T(1,128)S(1)}, s32[1,4]{1,0:T(1,128)}, u32[]{:S(2)}) copy-start(s32[1,4]{1,0:T(1,128)} %param.15) | copy-start | bytes 52
  11.3 11.6 %copy-start.9 = (f32[1,2]{1,0:T(1,128)S(1)}, f32[1,2]{1,0:T(1,128)}, u32[]{:S(2)}) copy-start(f32[1,2]{1,0:T(1,128)} %param.14) | copy-start | bytes 28
  12.7 25.0 %collective-permute-start = (f32[2,4,8,128]{2,3,1,0:T(8,128)}, f32[2,4,8,128]{2,3,1,0:T(8,128)}, u32[]{:S(2)}, u32[]{:S(2)}) collective-permute-start(f32[2,4,8,128]{2,3,1,0:T(8,128)} %get-tuple-element.15), channel_id=1, source_target_pairs={{0,4},{4,8},{8,12},{1,5},{5,9},{9,13},{2,6},{6,10},{10,14},{3,7},{... | collective-permute-start | bytes 98312 | tf_op jit(solution)/shard_map/ppermute | solution.py:17
  18.0 24.2 %collective-permute-start.1 = (f32[2,4,8,128]{2,3,1,0:T(8,128)}, f32[2,4,8,128]{2,3,1,0:T(8,128)}, u32[]{:S(2)}, u32[]{:S(2)}) collective-permute-start(f32[2,4,8,128]{2,3,1,0:T(8,128)} %get-tuple-element.16), channel_id=1, source_target_pairs={{4,0},{8,4},{12,8},{5,1},{9,5},{13,9},{6,2},{10,6},{14,10},{7,3},{... | collective-permute-start | bytes 98312 | tf_op jit(solution)/shard_map/ppermute | solution.py:19
  32.7 15.5 %copy-start = (f32[3,4,4,128]{2,3,1,0:T(8,128)S(1)}, f32[3,4,4,128]{2,3,1,0:T(8,128)}, u32[]{:S(2)}) copy-start(f32[3,4,4,128]{2,3,1,0:T(8,128)} %copy.43) | copy-start | bytes 73732
  32.7 15.4 %collective-permute-start.6 = (f32[3,4,264,4]{2,3,1,0:T(4,128)S(1)}, f32[3,4,264,4]{2,3,1,0:T(4,128)S(1)}, u32[]{:S(2)}, u32[]{:S(2)}) collective-permute-start(f32[3,4,264,4]{2,3,1,0:T(4,128)S(1)} %get-tuple-element.9), channel_id=1, source_target_pairs={{0,1},{1,2},{2,3},{4,5},{5,6},{6,7},{8,9},{9,10},{10,11},{12,13},{... | collective-permute-start | bytes 152072 | tf_op jit(solution)/shard_map/ppermute | solution.py:17
  36.3 11.8 %collective-permute-start.7 = (f32[3,4,264,4]{2,3,1,0:T(4,128)S(1)}, f32[3,4,264,4]{2,3,1,0:T(4,128)S(1)}, u32[]{:S(2)}, u32[]{:S(2)}) collective-permute-start(f32[3,4,264,4]{2,3,1,0:T(4,128)S(1)} %get-tuple-element.10), channel_id=1, source_target_pairs={{1,0},{2,1},{3,2},{5,4},{6,5},{7,6},{9,8},{10,9},{11,10},{13,12},{... | collective-permute-start | bytes 152072 | tf_op jit(solution)/shard_map/ppermute | solution.py:19
  43.2 8.7 %collective-permute-start.2 = (f32[2,4,272,8]{2,3,1,0:T(8,128)S(1)}, f32[2,4,272,8]{2,3,1,0:T(8,128)S(1)}, u32[]{:S(2)}, u32[]{:S(2)}) collective-permute-start(f32[2,4,272,8]{2,3,1,0:T(8,128)S(1)} %get-tuple-element.12), channel_id=1, source_target_pairs={{0,1},{1,2},{2,3},{4,5},{5,6},{6,7},{8,9},{9,10},{10,11},{12,13},{... | collective-permute-start | bytes 208904 | tf_op jit(solution)/shard_map/ppermute | solution.py:17
  46.7 6.5 %collective-permute-start.3 = (f32[2,4,272,8]{2,3,1,0:T(8,128)S(1)}, f32[2,4,272,8]{2,3,1,0:T(8,128)S(1)}, u32[]{:S(2)}, u32[]{:S(2)}) collective-permute-start(f32[2,4,272,8]{2,3,1,0:T(8,128)S(1)} %get-tuple-element.11), channel_id=1, source_target_pairs={{1,0},{2,1},{3,2},{5,4},{6,5},{7,6},{9,8},{10,9},{11,10},{13,12},{... | collective-permute-start | bytes 208904 | tf_op jit(solution)/shard_map/ppermute | solution.py:19
  53.2 0.6 copy-start.6
  55.6 1.0 copy-start.2
  55.6 1.0 copy-start.7
  67.5 1.0 copy-start.1
  67.6 1.1 copy-start.3
